TPU v7x, 256 devices: a whole 4x4x8 slice. The times are simulated.
256 devices in a mesh: seq: 16 (over y_lo, z), dp: 16 (over x, y_hi, core).
Axes of the slice: x: 4, y: 4 (y_hi: 2, y_lo: 2; y = y_hi * 2 + y_lo), z: 8, core: 2. Of those that a mesh axis runs over, the one named last changes fastest.
Arguments:
- layer_rows: bfloat16 [16, 2048, 1024], P('dp', 'seq'), may hold values from -6 to 6
- doc_ids: int32 [16, 2048], P('dp', 'seq'), may hold values from 0 to 5, never falling along the last dimension, each value on 1 to 1024 neighbouring positions
- packing: int32 [16, 16], P('dp'), may hold values from 0 to 15, each once within a row
- norm_gain: float32 [1024], replicated, may hold values from 0.1 to 1.9
- w_qkv: bfloat16 [1024, 3072], replicated, may hold values from -0.1875 to 0.1875
- d_attn: bfloat16 [16, 2048, 1024], P('dp', 'seq'), may hold values from -6 to 6
Outputs:
- d_input: bfloat16 [16, 2048, 1024], P('dp', 'seq')
- w_grad: float32 [1024, 3072], P('seq')
Inputs may be any that keep to these rules, and one draw needn't show every extreme that they name: `doc_ids`: in each group the song numbers never fall along the initial order; every number occurs, and one song spans exactly 1024 frames. `packing`: each group's row names every block number once.
All inputs are finite; a program needn't handle non-finite values.
Results may differ from a plain program's by a relative error of at most 0.024.
Values may be sent and summed in bfloat16 or wider, within the bound.
No kernel may reach another device: no remote copies, remote signals or barrier semaphores. Data moves between devices by JAX's collectives and lax.ppermute only.
A program may use at most 128 MiB of HBM per device.

v0:
```python
import math
import jax
import jax.numpy as jnp
from jax import lax
from jax.sharding import PartitionSpec as P

HEADS = 8
HEAD = 128
BLOCK = 128


def rounded(value):
    return lax.optimization_barrier(value.astype(jnp.bfloat16)).astype(jnp.float32)


def normalize(frames, norm_gain):
    values = frames.astype(jnp.float32)
    inverse = lax.rsqrt(jnp.mean(values * values, axis=-1, keepdims=True) + 1e-05)
    unit_rows = values * inverse
    return (inverse, unit_rows, (unit_rows * norm_gain).astype(jnp.bfloat16))


def body(layer_rows, doc_ids, packing, norm_gain, w_qkv, d_attn):
    shards = lax.axis_size("seq")
    my_index = lax.axis_index("seq")
    frames = layer_rows[0]
    tok_rows = frames.shape[0]
    head_cols = HEADS * HEAD
    total_keys = tok_rows * shards
    block_order = packing[0]
    key_pos = (block_order[:, None] * BLOCK + jnp.arange(BLOCK, dtype=jnp.int32)[None, :]).reshape(
        total_keys
    )
    first_own = my_index * tok_rows
    my_pos = lax.dynamic_slice_in_dim(key_pos, first_own, tok_rows, 0)
    doc_low = doc_ids[0].astype(jnp.bfloat16)
    pieces = (
        lax.all_gather(frames, "seq", axis=0, tiled=True),
        lax.all_gather(doc_low, "seq", axis=0, tiled=True),
    )
    length = pieces[0].shape[0]
    inside = (my_pos >= 0) & (my_pos < length)
    clipped = jnp.clip(my_pos, 0, length - 1)
    new_rows = jnp.where(
        inside[:, None], jnp.take(pieces[0], clipped, axis=0), jnp.zeros_like(frames)
    )
    new_docs = jnp.where(inside, jnp.take(pieces[1], clipped, axis=0), jnp.zeros_like(doc_low))
    inverse, unit_rows, normed = normalize(new_rows, norm_gain)
    projected = jnp.dot(normed, w_qkv, preferred_element_type=jnp.float32).astype(jnp.bfloat16)
    queries = projected[:, :head_cols]
    all_keys, all_values, key_docs_low = (
        lax.all_gather(projected[:, head_cols : 2 * head_cols], "seq", axis=0, tiled=True),
        lax.all_gather(projected[:, 2 * head_cols :], "seq", axis=0, tiled=True),
        lax.all_gather(new_docs, "seq", axis=0, tiled=True),
    )
    key_docs = key_docs_low.astype(jnp.int32)
    my_docs = lax.dynamic_slice_in_dim(key_docs, first_own, tok_rows, 0)
    factor = 1.0 / math.sqrt(HEAD)
    q_heads = queries.reshape(tok_rows, HEADS, HEAD)
    grad_heads = d_attn[0].reshape(tok_rows, HEADS, HEAD)
    group_count = total_keys // total_keys

    def key_slab(group_idx):
        first_key = group_idx * total_keys
        slab_keys = all_keys.reshape(total_keys, HEADS, HEAD)
        slab_values = all_values.reshape(total_keys, HEADS, HEAD)
        allowed = (my_docs[:, None] == key_docs[None, :]) & (key_pos[None, :] <= my_pos[:, None])
        return (first_key, slab_keys, slab_values, allowed)

    def exp_scores(query_part, slab_keys, allowed):
        scores = (
            jnp.einsum("qhd,khd->hqk", query_part, slab_keys, preferred_element_type=jnp.float32)
            * factor
        )
        return jnp.where(allowed[None], jnp.exp(scores), jnp.float32(0.0))

    def add_denominator(group_idx, running):
        first_key, slab_keys, slab_values, allowed = key_slab(group_idx)
        return running + jnp.sum(exp_scores(q_heads, slab_keys, allowed), axis=-1)

    denominator = lax.fori_loop(
        0, group_count, add_denominator, jnp.zeros((HEADS, tok_rows), jnp.float32)
    )

    def probabilities(slab_keys, allowed):
        attn_prob = exp_scores(q_heads, slab_keys, allowed) / denominator[:, :, None]
        return (attn_prob, attn_prob.astype(jnp.bfloat16))

    def add_output(group_idx, running):
        first_key, slab_keys, slab_values, allowed = key_slab(group_idx)

        def compute():
            attn_prob, prob_low = probabilities(slab_keys, allowed)
            return jnp.einsum(
                "hqk,khd->qhd", prob_low, slab_values, preferred_element_type=jnp.float32
            )

        return running + compute()

    outputs = lax.fori_loop(
        0, group_count, add_output, jnp.zeros((tok_rows, HEADS, HEAD), jnp.float32)
    )
    row_delta = jnp.sum(grad_heads.astype(jnp.float32) * outputs, axis=-1).T

    def slab_backward(slab_keys, slab_values, allowed):
        attn_prob, prob_low = probabilities(slab_keys, allowed)
        grad_prob = jnp.einsum(
            "qhd,khd->hqk", grad_heads, slab_values, preferred_element_type=jnp.float32
        )
        dscore = (attn_prob * (grad_prob - row_delta[:, :, None])).astype(jnp.bfloat16)
        dq_part = (
            jnp.einsum("hqk,khd->qhd", dscore, slab_keys, preferred_element_type=jnp.float32)
            * factor
        )
        return (dq_part, dscore, prob_low)

    def add_grads(group_idx, running):
        dq_sum, kv_grads = running
        first_key, slab_keys, slab_values, allowed = key_slab(group_idx)

        def compute():
            dq_part, dscore, prob_low = slab_backward(slab_keys, slab_values, allowed)
            dk_part = (
                jnp.einsum("hqk,qhd->khd", dscore, q_heads, preferred_element_type=jnp.float32)
                * factor
            )
            dv_part = jnp.einsum(
                "hqk,qhd->khd", prob_low, grad_heads, preferred_element_type=jnp.float32
            )
            return (
                dq_part,
                jnp.concatenate(
                    [
                        dk_part.reshape(total_keys, head_cols),
                        dv_part.reshape(total_keys, head_cols),
                    ],
                    axis=1,
                ),
            )

        dq_part, kv_part = compute()
        return (dq_sum + dq_part, kv_part)

    dq_sum, kv_grads = lax.fori_loop(
        0,
        group_count,
        add_grads,
        (
            jnp.zeros((tok_rows, HEADS, HEAD), jnp.float32),
            jnp.zeros((total_keys, 2 * head_cols), jnp.float32),
        ),
    )
    summed = lax.psum_scatter(
        rounded(kv_grads).astype(jnp.bfloat16), "seq", scatter_dimension=0, tiled=True
    ).astype(jnp.float32)
    grad_qkv = jnp.concatenate([dq_sum.reshape(tok_rows, head_cols), summed], axis=1).astype(
        jnp.bfloat16
    )
    d_normed = lax.dot_general(
        grad_qkv, w_qkv, (((1,), (1,)), ((), ())), preferred_element_type=jnp.float32
    )
    gained = d_normed * norm_gain
    d_frames = (
        inverse * (gained - unit_rows * jnp.mean(gained * unit_rows, axis=-1, keepdims=True))
    ).astype(jnp.bfloat16)
    w_part = lax.psum_scatter(
        rounded(
            lax.dot_general(
                normed, grad_qkv, (((0,), (0,)), ((), ())), preferred_element_type=jnp.float32
            )
        ).astype(jnp.bfloat16),
        "seq",
        scatter_dimension=0,
        tiled=True,
    )
    w_total = lax.psum(w_part, "dp").astype(jnp.float32)
    w_grad = w_total * (1.0 / math.sqrt(total_keys * lax.axis_size("dp")))
    return (d_frames[None], w_grad)


def solution(mesh):
    return jax.shard_map(
        body,
        mesh=mesh,
        in_specs=(
            P("dp", "seq", None),
            P("dp", "seq"),
            P("dp", None),
            P(),
            P(),
            P("dp", "seq", None),
        ),
        out_specs=(P("dp", "seq", None), P("seq", None)),
        check_vma=False,
    )
```

profile of v0, /device:TPU:1, one launch (start us, length us, event | category | flops | bytes accessed | tf_op | source)
XLA Modules:
  0.0 635.3 jit_solution(11670641613337491043)
XLA Ops:
  7.2 0.0 all-gather.11.cloned.1.call-start
  7.2 0.7 all-gather.11.cloned.1.call-update
  7.9 0.0 all-gather.7.cloned.1.call-start
  7.9 0.7 multiply_bitcast_fusion
  8.6 0.1 add_bitcast_fusion
  8.7 0.1 compare_and_fusion.2
  8.8 71.3 %all-gather.11.cloned.1.call-done = bf16[1,2048,1024]{2,1,0:T(8,128)(2,1)} async-done(((bf16[1,128,1024]{2,1,0:T(8,128)(2,1)}), bf16[1,2048,1024]{2,1,0:T(8,128)(2,1)}) %all-gather.11.cloned.1.call-update) | async-done | bytes 4194320 | tf_op jit(solution)/shard_map/all_gather | solution.py:38
  80.1 3.8 gather_fusion
  83.8 0.2 fusion.24
  84.1 0.0 copy-start.5
  84.1 0.0 copy-start.3
  84.1 3.9 convolution_convert_fusion.2
  88.1 0.8 fusion.32
  88.9 0.0 all-gather.7.cloned.1.call-update
  88.9 0.0 all-gather.9.cloned.1.call-start
  89.0 0.7 all-gather.9.cloned.1.call-update
  89.7 0.0 reduce-scatter.7.cloned.1.call-start
  89.7 0.0 copy-done.5
  89.7 25.4 %all-gather.1 = bf16[1,2048]{1,0:T(2,128)(2,1)S(1)} all-gather(bf16[1,128]{1,0:T(2,128)(2,1)S(1)} %convert_element_type.50), channel_id=3, replica_groups=mesh['seq'=16,'dp'=16] {'seq'}, dimensions={1}, use_global_device_ids=true | all-gather | bytes 4352 | tf_op jit(solution)/shard_map/all_gather | solution.py:39
  115.2 1.3 gather_fusion.1
  116.5 24.9 %all-gather.2 = bf16[16,1,128]{2,1,0:T(2,128)(2,1)S(1)} all-gather(bf16[1,1,128]{2,1,0:T(2,128)(2,1)S(1)} %select_bitcast_fusion), channel_id=1, replica_groups=mesh['seq'=16,'dp'=16] {'seq'}, dimensions={0}, use_global_device_ids=true | all-gather | bytes 4352 | tf_op jit(solution)/shard_map/all_gather | solution.py:54
  141.5 0.1 dynamic_slice.7
  141.5 0.0 copy-done.3
  141.5 0.2 copy.28
  141.7 0.3 compare_and_fusion
  142.0 0.2 copy.40
  142.2 21.2 %all-gather.7.cloned.1.call-done = bf16[2048,1024]{1,0:T(8,128)(2,1)} async-done(((bf16[128,1024]{1,0:T(8,128)(2,1)}), bf16[2048,1024]{1,0:T(8,128)(2,1)}) %all-gather.7.cloned.1.call-update) | async-done | bytes 4194320 | tf_op jit(solution)/shard_map/all_gather | solution.py:52
  163.4 6.5 %copy.39 = bf16[2048,1024]{0,1:T(8,128)(2,1)} copy(bf16[2048,1024]{1,0:T(8,128)(2,1)} %all-gather.7.cloned.1.call-done) | data formatting | bytes 8388608 | tf_op jit(solution)/shard_map/while/body/eval_jaxpr/reshape | solution.py:65
  169.9 5.1 fusion.2
  175.0 0.0 copy-start
  175.0 3.2 copy-done
  178.2 4.5 convolution_convert_fusion.1
  182.8 55.8 %all-gather.9.cloned.1.call-done = bf16[2048,1024]{1,0:T(8,128)(2,1)} async-done(((bf16[128,1024]{1,0:T(8,128)(2,1)}), bf16[2048,1024]{1,0:T(8,128)(2,1)}) %all-gather.9.cloned.1.call-update) | async-done | bytes 4194320 | tf_op jit(solution)/shard_map/all_gather | solution.py:53
  238.5 6.5 %copy.41 = bf16[2048,1024]{0,1:T(8,128)(2,1)} copy(bf16[2048,1024]{1,0:T(8,128)(2,1)} %all-gather.9.cloned.1.call-done) | data formatting | bytes 8388608 | tf_op jit(solution)/shard_map/while/body/eval_jaxpr/reshape | solution.py:66
  245.0 0.0 copy-start.1
  245.0 7.3 %fusion.13 = f32[128,8]{0,1:T(8,128)S(1)} fusion(bf16[2048,8,128]{0,2,1:T(8,128)(2,1)} %bitcast.50, bf16[128,8,128]{0,2,1:T(8,128)(2,1)S(1)} %bitcast.59, f32[8,128,2048]{2,1,0:T(8,128)} %copy-done, f32[8,128]{1,0:T(8,128)S(1)} %get-tuple-element.73, pred[128,2048]{1,0:T(8,128)(4,1)S(1)} %compare_and_fusion), kind=kOutput, calls=%fused_computation.20 | convolution fusion | flops 545651712 | bytes 13115392 | tf_op jit(solution)/shard_map/while/body/eval_jaxpr/hqk,khd->qhd/dot_general | solution.py:94
  252.3 0.0 copy-done.1
  252.3 5.2 fusion
  257.6 0.0 copy-start.2
  257.6 2.0 copy-done.2
  259.5 3.2 multiply_convert_fusion
  262.7 8.3 %pad_maximum_fusion = bf16[2048,2048]{0,1:T(8,128)(2,1)} fusion(bf16[2048,1024]{0,1:T(8,128)(2,1)} %bitcast.52, bf16[2048,1024]{0,1:T(8,128)(2,1)} %bitcast.49), kind=kLoop, calls=%fused_computation.2 | loop fusion | flops 16777216 | bytes 16777216 | tf_op jit(solution)/shard_map/while/body/eval_jaxpr/concatenate | solution.py:132
  271.1 12.2 %copy.37 = bf16[2048,2048]{1,0:T(8,128)(2,1)} copy(bf16[2048,2048]{0,1:T(8,128)(2,1)} %pad_maximum_fusion) | data formatting | bytes 16777216
  283.3 0.0 reduce-scatter.7.cloned.1.call-update
  283.3 0.0 copy-start.4
  283.3 0.3 reduce-scatter.5.cloned.1.call-start
  283.6 4.7 fusion.12
  288.3 103.2 %reduce-scatter.7.cloned.1.call-done = bf16[128,2048]{1,0:T(8,128)(2,1)} async-done(((bf16[2048,2048]{1,0:T(8,128)(2,1)}), bf16[128,2048]{1,0:T(8,128)(2,1)}) %reduce-scatter.7.cloned.1.call-update) | async-done | bytes 524304
  391.6 1.3 copy.38
  392.9 0.0 copy-done.4
  392.9 4.6 convolution_convert_fusion
  397.5 0.0 reduce-scatter.5.cloned.1.call-update
  397.6 0.0 all-reduce.2.cloned.1.call-start
  397.6 5.1 fusion.20
  402.7 71.0 %reduce-scatter.5.cloned.1.call-done = bf16[64,3072]{1,0:T(8,128)(2,1)} async-done(((bf16[1024,3072]{1,0:T(8,128)(2,1)}), bf16[64,3072]{1,0:T(8,128)(2,1)}) %reduce-scatter.5.cloned.1.call-update) | async-done | bytes 393232 | tf_op jit(solution)/shard_map/reduce_scatter | solution.py:166
  473.8 0.0 all-reduce.2.cloned.1.call-update
  473.8 0.9 fusion.25
  474.7 151.8 %all-reduce.2.cloned.1.call-done = bf16[64,3072]{1,0:T(8,128)(2,1)} async-done(((bf16[64,3072]{1,0:T(8,128)(2,1)}), bf16[64,3072]{1,0:T(8,128)(2,1)}) %all-reduce.2.cloned.1.call-update) | async-done | bytes 393232 | tf_op jit(solution)/shard_map/psum | solution.py:176
  626.5 1.9 convert_multiply_fusion
  (9 shorter events, 0.1 us)
Async XLA Ops:
  7.2 72.9 %all-gather.11.cloned.1.call-start = ((), (), s32[]{:S(2)}) async-start(), calls=%async_computation.6 | async-start | bytes 4456448 | tf_op jit(solution)/shard_map/all_gather | solution.py:38
  7.9 155.5 %all-gather.7.cloned.1.call-start = ((), (), s32[]{:S(2)}) async-start(), calls=%async_computation.2 | async-start | bytes 4456448 | tf_op jit(solution)/shard_map/all_gather | solution.py:52
  84.1 5.6 copy-start.5
  84.1 57.4 %copy-start.3 = (bf16[1,128,1024]{2,1,0:T(8,128)(2,1)S(1)}, bf16[1,128,1024]{2,1,0:T(8,128)(2,1)}, u32[]{:S(2)}) copy-start(bf16[1,128,1024]{2,1,0:T(8,128)(2,1)} %param.11) | copy-start | bytes 786436
  88.9 149.6 %all-gather.9.cloned.1.call-start = ((), (), s32[]{:S(2)}) async-start(), calls=%async_computation.3 | async-start | bytes 4456448 | tf_op jit(solution)/shard_map/all_gather | solution.py:53
  89.7 301.9 %reduce-scatter.7.cloned.1.call-start = ((), (), s32[]{:S(2)}) async-start(), calls=%async_computation.7 | async-start | bytes 8912896
  175.0 3.2 copy-start
  245.0 7.3 %copy-start.1 = (f32[8,128,2048]{2,1,0:T(8,128)S(1)}, f32[8,128,2048]{2,1,0:T(8,128)}, u32[]{:S(2)}) copy-start(f32[8,128,2048]{2,1,0:T(8,128)} %copy-done) | copy-start | bytes 25165828
  257.6 2.0 copy-start.2
  283.3 109.6 %copy-start.4 = (f32[1024]{0:T(1024)S(1)}, f32[1024]{0:T(1024)}, u32[]{:S(2)}) copy-start(f32[1024]{0:T(1024)} %param.9) | copy-start | bytes 12292
  283.3 190.4 %reduce-scatter.5.cloned.1.call-start = ((), (), s32[]{:S(2)}) async-start(), calls=%async_computation.4 | async-start | bytes 6684672 | tf_op jit(solution)/shard_map/reduce_scatter | solution.py:166
  397.6 228.9 %all-reduce.2.cloned.1.call-start = ((), (), s32[]{:S(2)}) async-start(), calls=%async_computation.5 | async-start | bytes 786432 | tf_op jit(solution)/shard_map/psum | solution.py:176
Sparse Core Ops, SparseCore 0:
  9.8 70.2 all-gather.10
  89.0 74.2 all-gather.6
  165.7 72.7 all-gather.8
  283.5 108.0 reduce-scatter.6
  397.7 76.0 reduce-scatter.4
  476.2 150.2 all-reduce.1
where the time goes:
time: 636 us; the launch traced here: 635 us
  waiting for transfers between devices  476 us (75%)
  blocking collectives  50.4 us (8%)
  matrix products  43.7 us (7%)
  local copies, waits for them, and re-layouts  38.1 us (6%)
  between operations  14.3 us (2%)
  other arithmetic  12.6 us (2%)
    psum x1, waiting for transfers between devices, body(): w_total = lax.psum(w_part, 'dp').astype(jnp.float32)  152 us
    unnamed x7, waiting for transfers between devices  105 us
    all_gather x1, waiting for transfers between devices, body(): lax.all_gather(frames, 'seq', axis=0, tiled=True)  71.3 us
    reduce_scatter x1, waiting for transfers between devices, body(): lax.psum_scatter(rounded(lax.dot_general(normed, grad_qkv, (((0,), (0,)),...  71 us
    all_gather x1, waiting for transfers between devices, body(): lax.all_gather(projected[:, 2 * head_cols:], 'seq', axis=0, tiled=True)  55.8 us
    all_gather x1, blocking collectives, body(): lax.all_gather(doc_low, 'seq', axis=0, tiled=True)  25.4 us
    all_gather x1, blocking collectives, body(): lax.all_gather(new_docs, 'seq', axis=0, tiled=True)  24.9 us
    all_gather x1, waiting for transfers between devices, body(): lax.all_gather(projected[:, head_cols:2 * head_cols], 'seq', axis=0, tile...  21.2 us
  transfers between devices with their start and end apart: 6, of which 6 were waited for; matrix products, arithmetic and copies ran while one was open for 5% of the time, Pallas kernels for 0%

commit v1 on v0

--- a/solution.py
+++ b/solution.py
@@ -173,7 +173,7 @@
         scatter_dimension=0,
         tiled=True,
     )
-    w_total = lax.psum(w_part, "dp").astype(jnp.float32)
+    w_total = jnp.sum(lax.all_gather(w_part, "dp"), axis=0).astype(jnp.float32)
     w_grad = w_total * (1.0 / math.sqrt(total_keys * lax.axis_size("dp")))
     return (d_frames[None], w_grad)
 

time: 636 us -> 564 us (0.89)
  waiting for transfers between devices: 476 us -> 401 us
    psum x1 -> x0, waiting for transfers between devices: 152 us -> none  [body(): w_total = lax.psum(w_part, 'dp').astype(jnp.float32)]
    all_gather x0 -> x1, waiting for transfers between devices: none -> 71.8 us  [body(): w_total = jnp.sum(lax.all_gather(w_part, 'dp'), axis=0).astype(jnp.float32)]
where the time goes in v1:
time: 564 us; the launch traced here: 563 us
  waiting for transfers between devices  401 us (71%)
  blocking collectives  50.4 us (9%)
  matrix products  43.7 us (8%)
  local copies, waits for them, and re-layouts  38.1 us (7%)
  other arithmetic  15.6 us (3%)
  between operations  14.3 us (3%)
    unnamed x7, waiting for transfers between devices  105 us
    reduce_scatter x1, waiting for transfers between devices, body(): lax.psum_scatter(rounded(lax.dot_general(normed, grad_qkv, (((0,), (0,)),...  76.1 us
    all_gather x1, waiting for transfers between devices, body(): w_total = jnp.sum(lax.all_gather(w_part, 'dp'), axis=0).astype(jnp.float32)  71.8 us
    all_gather x1, waiting for transfers between devices, body(): lax.all_gather(frames, 'seq', axis=0, tiled=True)  71.3 us
    all_gather x1, waiting for transfers between devices, body(): lax.all_gather(projected[:, 2 * head_cols:], 'seq', axis=0, tiled=True)  55.8 us
    all_gather x1, blocking collectives, body(): lax.all_gather(doc_low, 'seq', axis=0, tiled=True)  25.4 us
    all_gather x1, blocking collectives, body(): lax.all_gather(new_docs, 'seq', axis=0, tiled=True)  24.9 us
    all_gather x1, waiting for transfers between devices, body(): lax.all_gather(projected[:, head_cols:2 * head_cols], 'seq', axis=0, tile...  21.2 us
  transfers between devices with their start and end apart: 6, of which 6 were waited for; matrix products, arithmetic and copies ran while one was open for 5% of the time, Pallas kernels for 0%

profile of v1, /device:TPU:1, one launch (start us, length us, event | category | flops | bytes accessed | tf_op | source)
XLA Modules:
  0.0 563.4 jit_solution(12293362231171546904)
XLA Ops:
  7.2 0.0 all-gather.13.cloned.1.call-start
  7.2 0.7 all-gather.13.cloned.1.call-update
  7.9 0.0 all-gather.9.cloned.1.call-start
  7.9 0.7 multiply_bitcast_fusion
  8.6 0.1 add_bitcast_fusion
  8.7 0.1 compare_and_fusion.2
  8.8 71.3 %all-gather.13.cloned.1.call-done = bf16[1,2048,1024]{2,1,0:T(8,128)(2,1)} async-done(((bf16[1,128,1024]{2,1,0:T(8,128)(2,1)}), bf16[1,2048,1024]{2,1,0:T(8,128)(2,1)}) %all-gather.13.cloned.1.call-update) | async-done | bytes 4194320 | tf_op jit(solution)/shard_map/all_gather | solution.py:38
  80.1 3.8 gather_fusion
  83.8 0.2 fusion.24
  84.1 0.0 copy-start.5
  84.1 0.0 copy-start.3
  84.1 3.9 convolution_convert_fusion.2
  88.1 0.8 fusion.32
  88.9 0.0 all-gather.9.cloned.1.call-update
  88.9 0.0 all-gather.11.cloned.1.call-start
  89.0 0.7 all-gather.11.cloned.1.call-update
  89.7 0.0 reduce-scatter.7.cloned.1.call-start
  89.7 0.0 copy-done.5
  89.7 25.4 %all-gather.1 = bf16[1,2048]{1,0:T(2,128)(2,1)S(1)} all-gather(bf16[1,128]{1,0:T(2,128)(2,1)S(1)} %convert_element_type.52), channel_id=3, replica_groups=mesh['seq'=16,'dp'=16] {'seq'}, dimensions={1}, use_global_device_ids=true | all-gather | bytes 4352 | tf_op jit(solution)/shard_map/all_gather | solution.py:39
  115.2 1.3 gather_fusion.1
  116.5 24.9 %all-gather.3 = bf16[16,1,128]{2,1,0:T(2,128)(2,1)S(1)} all-gather(bf16[1,1,128]{2,1,0:T(2,128)(2,1)S(1)} %select_bitcast_fusion), channel_id=1, replica_groups=mesh['seq'=16,'dp'=16] {'seq'}, dimensions={0}, use_global_device_ids=true | all-gather | bytes 4352 | tf_op jit(solution)/shard_map/all_gather | solution.py:54
  141.5 0.1 dynamic_slice.7
  141.5 0.0 copy-done.3
  141.5 0.2 copy.28
  141.7 0.3 compare_and_fusion
  142.0 0.2 copy.40
  142.2 21.2 %all-gather.9.cloned.1.call-done = bf16[2048,1024]{1,0:T(8,128)(2,1)} async-done(((bf16[128,1024]{1,0:T(8,128)(2,1)}), bf16[2048,1024]{1,0:T(8,128)(2,1)}) %all-gather.9.cloned.1.call-update) | async-done | bytes 4194320 | tf_op jit(solution)/shard_map/all_gather | solution.py:52
  163.4 6.5 %copy.39 = bf16[2048,1024]{0,1:T(8,128)(2,1)} copy(bf16[2048,1024]{1,0:T(8,128)(2,1)} %all-gather.9.cloned.1.call-done) | data formatting | bytes 8388608 | tf_op jit(solution)/shard_map/while/body/eval_jaxpr/reshape | solution.py:65
  169.9 5.1 fusion.2
  175.0 0.0 copy-start
  175.0 3.2 copy-done
  178.2 4.5 convolution_convert_fusion.1
  182.8 55.8 %all-gather.11.cloned.1.call-done = bf16[2048,1024]{1,0:T(8,128)(2,1)} async-done(((bf16[128,1024]{1,0:T(8,128)(2,1)}), bf16[2048,1024]{1,0:T(8,128)(2,1)}) %all-gather.11.cloned.1.call-update) | async-done | bytes 4194320 | tf_op jit(solution)/shard_map/all_gather | solution.py:53
  238.5 6.5 %copy.41 = bf16[2048,1024]{0,1:T(8,128)(2,1)} copy(bf16[2048,1024]{1,0:T(8,128)(2,1)} %all-gather.11.cloned.1.call-done) | data formatting | bytes 8388608 | tf_op jit(solution)/shard_map/while/body/eval_jaxpr/reshape | solution.py:66
  245.0 0.0 copy-start.1
  245.0 7.3 %fusion.13 = f32[128,8]{0,1:T(8,128)S(1)} fusion(bf16[2048,8,128]{0,2,1:T(8,128)(2,1)} %bitcast.52, bf16[128,8,128]{0,2,1:T(8,128)(2,1)S(1)} %bitcast.61, f32[8,128,2048]{2,1,0:T(8,128)} %copy-done, f32[8,128]{1,0:T(8,128)S(1)} %get-tuple-element.73, pred[128,2048]{1,0:T(8,128)(4,1)S(1)} %compare_and_fusion), kind=kOutput, calls=%fused_computation.20 | convolution fusion | flops 545651712 | bytes 13115392 | tf_op jit(solution)/shard_map/while/body/eval_jaxpr/hqk,khd->qhd/dot_general | solution.py:94
  252.3 0.0 copy-done.1
  252.3 5.2 fusion
  257.6 0.0 copy-start.2
  257.6 2.0 copy-done.2
  259.5 3.2 multiply_convert_fusion
  262.7 8.3 %pad_maximum_fusion = bf16[2048,2048]{0,1:T(8,128)(2,1)} fusion(bf16[2048,1024]{0,1:T(8,128)(2,1)} %bitcast.54, bf16[2048,1024]{0,1:T(8,128)(2,1)} %bitcast.50), kind=kLoop, calls=%fused_computation.2 | loop fusion | flops 16777216 | bytes 16777216 | tf_op jit(solution)/shard_map/while/body/eval_jaxpr/concatenate | solution.py:132
  271.1 12.2 %copy.37 = bf16[2048,2048]{1,0:T(8,128)(2,1)} copy(bf16[2048,2048]{0,1:T(8,128)(2,1)} %pad_maximum_fusion) | data formatting | bytes 16777216
  283.3 0.0 reduce-scatter.7.cloned.1.call-update
  283.3 0.0 copy-start.4
  283.3 0.3 reduce-scatter.5.cloned.1.call-start
  283.6 4.7 fusion.12
  288.3 103.2 %reduce-scatter.7.cloned.1.call-done = bf16[128,2048]{1,0:T(8,128)(2,1)} async-done(((bf16[2048,2048]{1,0:T(8,128)(2,1)}), bf16[128,2048]{1,0:T(8,128)(2,1)}) %reduce-scatter.7.cloned.1.call-update) | async-done | bytes 524304
  391.6 1.3 copy.38
  392.9 0.0 copy-done.4
  392.9 4.6 convolution_convert_fusion
  397.5 0.0 reduce-scatter.5.cloned.1.call-update
  397.6 0.0 all-gather.15.cloned.1.call-start
  397.6 76.1 %reduce-scatter.5.cloned.1.call-done = bf16[64,3072]{1,0:T(8,128)(2,1)} async-done(((bf16[1024,3072]{1,0:T(8,128)(2,1)}), bf16[64,3072]{1,0:T(8,128)(2,1)}) %reduce-scatter.5.cloned.1.call-update) | async-done | bytes 393232 | tf_op jit(solution)/shard_map/reduce_scatter | solution.py:166
  473.8 0.0 all-gather.15.cloned.1.call-update
  473.8 5.1 fusion.20
  478.9 0.9 fusion.25
  479.8 71.8 %all-gather.15.cloned.1.call-done = bf16[1024,3072]{1,0:T(8,128)(2,1)} async-done(((bf16[64,3072]{1,0:T(8,128)(2,1)}), bf16[1024,3072]{1,0:T(8,128)(2,1)}) %all-gather.15.cloned.1.call-update) | async-done | bytes 6291472 | tf_op jit(solution)/shard_map/all_gather | solution.py:176
  551.6 4.0 reduce_sum.53
  555.6 0.9 convert_multiply_fusion
  (9 shorter events, 0.1 us)
Async XLA Ops:
  7.2 72.9 %all-gather.13.cloned.1.call-start = ((), (), s32[]{:S(2)}) async-start(), calls=%async_computation.5 | async-start | bytes 4456448 | tf_op jit(solution)/shard_map/all_gather | solution.py:38
  7.9 155.5 %all-gather.9.cloned.1.call-start = ((), (), s32[]{:S(2)}) async-start(), calls=%async_computation.2 | async-start | bytes 4456448 | tf_op jit(solution)/shard_map/all_gather | solution.py:52
  84.1 5.6 copy-start.5
  84.1 57.4 %copy-start.3 = (bf16[1,128,1024]{2,1,0:T(8,128)(2,1)S(1)}, bf16[1,128,1024]{2,1,0:T(8,128)(2,1)}, u32[]{:S(2)}) copy-start(bf16[1,128,1024]{2,1,0:T(8,128)(2,1)} %param.11) | copy-start | bytes 786436
  88.9 149.6 %all-gather.11.cloned.1.call-start = ((), (), s32[]{:S(2)}) async-start(), calls=%async_computation.3 | async-start | bytes 4456448 | tf_op jit(solution)/shard_map/all_gather | solution.py:53
  89.7 301.9 %reduce-scatter.7.cloned.1.call-start = ((), (), s32[]{:S(2)}) async-start(), calls=%async_computation.7 | async-start | bytes 8912896
  175.0 3.2 copy-start
  245.0 7.3 %copy-start.1 = (f32[8,128,2048]{2,1,0:T(8,128)S(1)}, f32[8,128,2048]{2,1,0:T(8,128)}, u32[]{:S(2)}) copy-start(f32[8,128,2048]{2,1,0:T(8,128)} %copy-done) | copy-start | bytes 25165828
  257.6 2.0 copy-start.2
  283.3 109.6 %copy-start.4 = (f32[1024]{0:T(1024)S(1)}, f32[1024]{0:T(1024)}, u32[]{:S(2)}) copy-start(f32[1024]{0:T(1024)} %param.9) | copy-start | bytes 12292
  283.3 190.4 %reduce-scatter.5.cloned.1.call-start = ((), (), s32[]{:S(2)}) async-start(), calls=%async_computation.4 | async-start | bytes 6684672 | tf_op jit(solution)/shard_map/reduce_scatter | solution.py:166
  397.6 154.0 %all-gather.15.cloned.1.call-start = ((), (), s32[]{:S(2)}) async-start(), calls=%async_computation.6 | async-start | bytes 6684672 | tf_op jit(solution)/shard_map/all_gather | solution.py:176
Sparse Core Ops, SparseCore 0:
  9.8 70.2 all-gather.12
  89.0 74.2 all-gather.8
  165.7 72.7 all-gather.10
  283.5 108.0 reduce-scatter.6
  397.7 76.0 reduce-scatter.4
  476.3 75.2 all-gather.14
